TPU v7x, 32 devices: a whole 2x2x4 slice. The times are simulated.
32 devices in a mesh: row: 8 (over z, x), ch: 4 (over y, core).
Axes of the slice: x: 2, y: 2, z: 4, core: 2. Of those that a mesh axis runs over, the one named last changes fastest.
Arguments:
- pair_rep: bfloat16 [128, 8, 8], P('ch', 'row'), may hold values from -6 to 6
- residue_mask: int32 [8], replicated, may hold values 0 or 1
- chain_ids: int32 [8], replicated, may hold values from 0 to 3, never falling along the last dimension, each value on 1 to 4 neighbouring positions
- in_gain: float32 [2, 128], replicated, may hold values from 0.5 to 1.5
- in_bias: float32 [2, 128], replicated, may hold values from -3 to 3
- w_proj: bfloat16 [2, 128, 4, 128], P(None, None, None, 'ch'), may hold values from -0.5 to 0.5
- w_gate: bfloat16 [2, 128, 128], P(None, None, 'ch'), may hold values from -0.5 to 0.5
- pair_bias: float32 [2, 128], P(None, 'ch'), may hold values from -4 to 4
- out_gain: float32 [2, 128], P(None, 'ch'), may hold values from 0.5 to 1.5
- out_bias: float32 [2, 128], P(None, 'ch'), may hold values from -3 to 3
- w_out: bfloat16 [2, 128, 128], P(None, 'ch'), may hold values from -0.5 to 0.5
Outputs:
- pair_out: bfloat16 [128, 8, 8], P('ch', 'row')
Inputs may be any that keep to these rules, and one draw needn't show every extreme that they name: `chain_ids`: chain numbers never fall along the residues; each chain has 1 to 4 residues.
All inputs are finite; a program needn't handle non-finite values.
Results may differ from a plain program's by a relative error of at most 0.013.
Values may be sent and summed in bfloat16 or wider, within the bound.
A program may use at most 64 MiB of HBM per device.

v0:
```python
import jax
import jax.numpy as jnp
from jax import lax
from jax.sharding import PartitionSpec as P

epsilon = 1e-05


def channel_norm(values, norm_gain, norm_bias):
    mean_val = jnp.mean(values, axis=0)
    variance = jnp.mean(values * values, axis=0) - mean_val * mean_val
    return (values - mean_val) * lax.rsqrt(variance + epsilon) * norm_gain[
        :, None, None
    ] + norm_bias[:, None, None]


def prepare(
    pair_local, layer, in_gain, in_bias, w_proj, w_gate, pair_bias, mask_rows, mask_cols, same_chain
):
    full_pair = lax.all_gather(pair_local, "ch", axis=0, tiled=True)
    normed = channel_norm(full_pair.astype(jnp.float32), in_gain[layer], in_bias[layer]).astype(
        jnp.bfloat16
    )
    projected = jnp.einsum(
        "cij,cpd->pdij", normed, w_proj[layer], preferred_element_type=jnp.float32
    )
    pair_mask = mask_rows[:, None] * mask_cols[None, :]
    first_arm = (jax.nn.sigmoid(projected[0]) * projected[1] * pair_mask).astype(jnp.bfloat16)
    second_arm = (jax.nn.sigmoid(projected[2]) * projected[3] * pair_mask).astype(jnp.bfloat16)
    logits = jnp.einsum("cij,cd->dij", normed, w_gate[layer], preferred_element_type=jnp.float32)
    logits = logits + pair_bias[layer][:, None, None] * same_chain[None]
    return (first_arm, second_arm, jax.nn.sigmoid(logits))


def finish(product_sum, gating, layer, out_gain, out_bias, w_out):
    totals = lax.psum(
        (jnp.sum(product_sum, axis=0), jnp.sum(product_sum * product_sum, axis=0)), "ch"
    )
    channels = product_sum.shape[0] * lax.axis_size("ch")
    mean_val = totals[0] / channels
    variance = totals[1] / channels - mean_val * mean_val
    scaled = (product_sum - mean_val) * lax.rsqrt(variance + epsilon)
    normed = (scaled * out_gain[layer][:, None, None] + out_bias[layer][:, None, None]).astype(
        jnp.bfloat16
    )
    columns = w_out[layer]
    mixed = lax.psum_scatter(
        jnp.einsum("dij,dc->cij", normed, columns, preferred_element_type=jnp.float32).astype(
            jnp.bfloat16
        ),
        "ch",
        scatter_dimension=0,
        tiled=True,
    ).astype(jnp.float32)
    return gating * mixed


def body(
    pair_rep,
    residue_mask,
    chain_ids,
    in_gain,
    in_bias,
    w_proj,
    w_gate,
    pair_bias,
    out_gain,
    out_bias,
    w_out,
):
    rows_here = pair_rep.shape[1]
    row_start = lax.axis_index("row") * rows_here
    mask_cols = residue_mask.astype(jnp.float32)
    mask_rows = lax.dynamic_slice_in_dim(mask_cols, row_start, rows_here)
    chain_rows = lax.dynamic_slice_in_dim(chain_ids, row_start, rows_here)
    same_chain = (chain_rows[:, None] == chain_ids[None, :]).astype(jnp.float32)
    first_arm, second_arm, gating = prepare(
        pair_rep, 0, in_gain, in_bias, w_proj, w_gate, pair_bias, mask_rows, mask_cols, same_chain
    )
    product_sum = jnp.einsum(
        "cik,cjk->cij",
        first_arm,
        lax.all_gather(second_arm, "row", axis=1, tiled=True),
        preferred_element_type=jnp.float32,
    )
    middle = (
        pair_rep.astype(jnp.float32) + finish(product_sum, gating, 0, out_gain, out_bias, w_out)
    ).astype(jnp.bfloat16)
    in_first, in_second, in_gating = prepare(
        middle, 1, in_gain, in_bias, w_proj, w_gate, pair_bias, mask_rows, mask_cols, same_chain
    )
    exchanged_left = lax.all_to_all(in_first, "row", split_axis=2, concat_axis=1, tiled=True)
    left_rows = jnp.swapaxes(exchanged_left, 1, 2)
    in_product = jnp.einsum(
        "cik,ckj->cij",
        left_rows,
        lax.all_gather(in_second, "row", axis=1, tiled=True),
        preferred_element_type=jnp.float32,
    )
    update = finish(in_product, in_gating, 1, out_gain, out_bias, w_out)
    return (middle.astype(jnp.float32) + update).astype(jnp.bfloat16)


def solution(mesh):
    return jax.shard_map(
        body,
        mesh=mesh,
        in_specs=(
            P("ch", "row", None),
            P(),
            P(),
            P(),
            P(),
            P(None, None, None, "ch"),
            P(None, None, "ch"),
            P(None, "ch"),
            P(None, "ch"),
            P(None, "ch"),
            P(None, "ch", None),
        ),
        out_specs=P("ch", "row", None),
        check_vma=False,
    )
```

profile of v0, /device:TPU:0, one launch (start us, length us, event | category | flops | bytes accessed | tf_op | source)
XLA Modules:
  0.0 143.6 jit_solution(11897451887013223469)
XLA Ops:
  6.5 0.0 reduce-scatter.7.cloned.1.call-start
  6.5 0.8 copy.22
  7.3 6.2 %all_gather.12 = bf16[128,1,8]{2,1,0:T(2,128)(2,1)S(1)} all-gather(bf16[32,1,8]{2,1,0:T(2,128)(2,1)S(1)} %copy.22), channel_id=1, replica_groups=mesh['row'=8,'ch'=4] {'ch'}, dimensions={0}, use_global_device_ids=true | all-gather | bytes 2560 | tf_op jit(solution)/shard_map/all_gather | solution.py:20
  13.5 0.0 copy-start.6
  13.5 0.1 copy.23
  13.6 0.2 convert_reduce_fusion.1
  13.8 0.0 copy-start.9
  13.8 0.6 copy-done.9
  14.4 0.6 dynamic_slice.7
  15.0 0.6 broadcast_multiply_fusion
  15.7 0.0 copy-start.2
  15.7 0.0 copy-start.3
  15.7 0.6 copy-done.2
  16.3 0.0 copy-done.3
  16.4 0.0 copy-done.6
  16.4 0.2 convolution_bitcast_fusion.1
  16.5 0.1 fusion.56
  16.6 0.1 fusion.78
  16.7 27.0 %all_gather.13 = bf16[32,8,8]{0,2,1:T(8,128)(2,1)S(1)} all-gather(bf16[32,1,8]{0,2,1:T(8,128)(2,1)S(1)} %fusion.56), channel_id=1, replica_groups=mesh['row'=8,'ch'=4] {'row'}, dimensions={1}, use_global_device_ids=true | all-gather | bytes 4608 | tf_op jit(solution)/shard_map/all_gather | solution.py:83
  43.7 0.0 copy-start.7
  43.7 0.1 fusion.84
  43.8 5.7 %all-reduce.1 = (f32[1,8]{1,0:T(1,128)S(1)}, f32[1,8]{1,0:T(1,128)S(1)}) all-reduce(f32[1,8]{1,0:T(1,128)S(1)} %bitcast.174, f32[1,8]{1,0:T(1,128)S(1)} %bitcast.173), channel_id=1, replica_groups=mesh['row'=8,'ch'=4] {'ch'}, use_global_device_ids=true, to_apply=%region_5.0 | all-reduce | flops 16 | bytes 128 | tf_op jit(solution)/shard_map/psum | solution.py:36
  49.5 0.0 copy-start.4
  49.5 0.0 copy-start.5
  49.5 0.7 copy-done.4
  50.2 0.0 copy-done.5
  50.2 0.0 copy-done.7
  50.2 0.2 fusion.18
  50.4 0.7 copy.40
  51.1 0.0 copy-start.10
  51.1 0.0 reduce-scatter.7.cloned.1.call-update
  51.1 0.6 copy-done.10
  51.7 0.0 copy-start.1
  51.7 0.0 copy-start.8
  51.7 0.6 dynamic_slice.6
  52.3 0.1 copy-done.1
  52.4 0.6 compare_convert_fusion
  53.1 0.0 copy-start
  53.1 17.3 %reduce-scatter.7.cloned.1.call-done = bf16[32,8]{1,0:T(8,128)(2,1)} async-done(((bf16[128,8]{1,0:T(8,128)(2,1)}), bf16[32,8]{1,0:T(8,128)(2,1)}) %reduce-scatter.7.cloned.1.call-update) | async-done | bytes 528
  70.4 0.8 copy.41
  71.2 0.0 copy-done.8
  71.2 0.0 copy-done
  71.2 0.2 fusion.17
  71.4 0.1 copy.24
  71.5 5.2 %all_gather.14 = bf16[128,1,8]{2,1,0:T(2,128)(2,1)S(1)} all-gather(bf16[32,1,8]{2,1,0:T(2,128)(2,1)S(1)} %copy.24), channel_id=1, replica_groups=mesh['row'=8,'ch'=4] {'ch'}, dimensions={0}, use_global_device_ids=true | all-gather | bytes 2560 | tf_op jit(solution)/shard_map/all_gather | solution.py:20
  76.7 0.1 copy.25
  76.8 0.2 convert_reduce_fusion
  77.0 0.2 convolution_bitcast_fusion
  77.2 0.1 fusion.50
  77.2 0.6 copy.26
  77.9 5.5 %all-to-all-start = ((bf16[32,1,8]{0,1,2:T(2,128)(2,1)}), bf16[32,1,8]{0,1,2:T(2,128)(2,1)S(1)}, u32[]{:S(2)}, u32[]{:S(2)}) async-start(bf16[32,1,8]{0,1,2:T(2,128)(2,1)} %copy.26), calls=%async_computation | async-start | bytes 8192 | tf_op jit(solution)/shard_map/all_to_all | solution.py:92
  83.4 0.0 reduce-scatter.9.cloned.1.call-start
  83.4 26.6 %all_gather.15 = bf16[32,8,8]{0,2,1:T(8,128)(2,1)S(1)} all-gather(bf16[32,1,8]{0,2,1:T(8,128)(2,1)S(1)} %get-tuple-element.18), channel_id=1, replica_groups=mesh['row'=8,'ch'=4] {'row'}, dimensions={1}, use_global_device_ids=true | all-gather | bytes 4608 | tf_op jit(solution)/shard_map/all_gather | solution.py:97
  110.0 0.0 all-to-all-done
  110.1 0.1 fusion.83
  110.2 5.9 %all-reduce = (f32[1,8]{1,0:T(1,128)S(1)}, f32[1,8]{1,0:T(1,128)S(1)}) all-reduce(f32[1,8]{1,0:T(1,128)S(1)} %bitcast.176, f32[1,8]{1,0:T(1,128)S(1)} %bitcast.175), channel_id=1, replica_groups=mesh['row'=8,'ch'=4] {'ch'}, use_global_device_ids=true, to_apply=%region_12.0 | all-reduce | flops 16 | bytes 128 | tf_op jit(solution)/shard_map/psum | solution.py:36
  116.2 0.2 fusion.19
  116.4 0.7 copy.42
  117.1 0.0 reduce-scatter.9.cloned.1.call-update
  117.1 18.1 %reduce-scatter.9.cloned.1.call-done = bf16[32,8]{1,0:T(8,128)(2,1)} async-done(((bf16[128,8]{1,0:T(8,128)(2,1)}), bf16[32,8]{1,0:T(8,128)(2,1)}) %reduce-scatter.9.cloned.1.call-update) | async-done | bytes 528
  135.2 0.8 copy.43
  136.0 0.8 fusion.16
  (11 shorter events, 0.1 us)
Async XLA Ops:
  6.5 63.9 %reduce-scatter.7.cloned.1.call-start = ((), (), s32[]{:S(2)}) async-start(), calls=%async_computation.3 | async-start | bytes 40960
  13.5 2.8 %copy-start.6 = (bf16[2,128,4,32]{1,3,2,0:T(8,128)(2,1)S(1)}, bf16[2,128,4,32]{1,3,2,0:T(8,128)(2,1)}, u32[]{:S(2)}) copy-start(bf16[2,128,4,32]{1,3,2,0:T(8,128)(2,1)} %param.16) | copy-start | bytes 196612
  13.8 0.7 copy-start.9
  15.7 0.7 copy-start.2
  15.7 0.7 copy-start.3
  43.7 6.5 %copy-start.7 = (bf16[2,32,128]{2,1,0:T(8,128)(2,1)S(1)}, bf16[2,32,128]{2,1,0:T(8,128)(2,1)}, u32[]{:S(2)}) copy-start(bf16[2,32,128]{2,1,0:T(8,128)(2,1)} %param.21) | copy-start | bytes 49156
  49.5 0.7 copy-start.4
  49.5 0.7 copy-start.5
  51.1 0.7 copy-start.10
  51.7 0.7 copy-start.1
  51.7 19.4 %copy-start.8 = (bf16[2,128,32]{1,2,0:T(8,128)(2,1)S(1)}, bf16[2,128,32]{1,2,0:T(8,128)(2,1)}, u32[]{:S(2)}) copy-start(bf16[2,128,32]{1,2,0:T(8,128)(2,1)} %param.17) | copy-start | bytes 49156
  53.1 18.1 %copy-start = (bf16[32,1,8]{0,2,1:T(8,128)(2,1)S(1)}, bf16[32,1,8]{0,2,1:T(8,128)(2,1)}, u32[]{:S(2)}) copy-start(bf16[32,1,8]{0,2,1:T(8,128)(2,1)} %param.11) | copy-start | bytes 1540
  77.9 32.2 %all-to-all-start = ((bf16[32,1,8]{0,1,2:T(2,128)(2,1)}), bf16[32,1,8]{0,1,2:T(2,128)(2,1)S(1)}, u32[]{:S(2)}, u32[]{:S(2)}) async-start(bf16[32,1,8]{0,1,2:T(2,128)(2,1)} %copy.26), calls=%async_computation | async-start | bytes 8192 | tf_op jit(solution)/shard_map/all_to_all | solution.py:92
  83.4 51.9 %reduce-scatter.9.cloned.1.call-start = ((), (), s32[]{:S(2)}) async-start(), calls=%async_computation.4 | async-start | bytes 40960
Sparse Core Ops, SparseCore 0:
  51.2 19.1 reduce-scatter.6
  117.2 17.9 reduce-scatter.8
where the time goes:
time: 144 us
  blocking collectives  76.7 us (53%)
  waiting for transfers between devices  35.5 us (25%)
  between operations  13.5 us (9%)
  local copies, waits for them, and re-layouts  8.5 us (6%)
  starting transfers between devices  5.55 us (4%)
  other arithmetic  2.19 us (2%)
  matrix products  1.71 us (1%)
    unnamed x4, waiting for transfers between devices  35.5 us
    all_gather x1, blocking collectives, body(): lax.all_gather(second_arm, 'row', axis=1, tiled=True)  27 us
    all_gather x1, blocking collectives, body(): lax.all_gather(in_second, 'row', axis=1, tiled=True)  26.6 us
    psum x2, blocking collectives, finish(): lax.psum((jnp.sum(product_sum, axis=0), jnp.sum(product_sum * product_sum...  11.6 us
    all_gather x2, blocking collectives, prepare(): full_pair = lax.all_gather(pair_local, 'ch', axis=0, tiled=True)  11.5 us
    unnamed x27, local copies, waits for them, and re-layouts  6.47 us
    all_to_all x1, starting transfers between devices, body(): lax.all_to_all(in_first, 'row', split_axis=2, concat_axis=1, tiled=True)  5.51 us
  transfers between devices with their start and end apart: 3, of which 2 were waited for; matrix products, arithmetic and copies ran while one was open for 1% of the time, Pallas kernels for 0%

commit v1 on v0

--- a/solution.py
+++ b/solution.py
@@ -17,7 +17,13 @@
 def prepare(
     pair_local, layer, in_gain, in_bias, w_proj, w_gate, pair_bias, mask_rows, mask_cols, same_chain
 ):
-    full_pair = lax.all_gather(pair_local, "ch", axis=0, tiled=True)
+    devices = lax.axis_size("ch")
+    moving, blocks = (pair_local, [pair_local])
+    for _ in range(devices - 1):
+        moving = lax.ppermute(moving, "ch", [(i, (i + 1) % devices) for i in range(devices)])
+        blocks.insert(0, moving)
+    merged = jnp.concatenate(blocks, axis=0)
+    full_pair = jnp.roll(merged, (lax.axis_index("ch") + 1) * pair_local.shape[0], axis=0)
     normed = channel_norm(full_pair.astype(jnp.float32), in_gain[layer], in_bias[layer]).astype(
         jnp.bfloat16
     )

time: 144 us -> 149 us (1.035)
  waiting for transfers between devices: 35.5 us -> 48.1 us
  blocking collectives: 76.7 us -> 65.3 us
  starting transfers between devices: 5.55 us -> 9.05 us
    all_gather x2 -> x0, blocking collectives: 11.5 us -> none  [prepare(): full_pair = lax.all_gather(pair_local, 'ch', axis=0, tiled=True)]
    ppermute x0 -> x6, waiting for transfers between devices: none -> 11.3 us  [prepare(): lax.ppermute(moving, 'ch', [(i, (i + 1) % devices) for i in range(devices)])]
    ppermute x0 -> x6, starting transfers between devices: none -> 3.5 us  [prepare(): lax.ppermute(moving, 'ch', [(i, (i + 1) % devices) for i in range(devices)])]
    unnamed x27 -> x26, local copies, waits for them, and re-layouts: 6.47 us -> 5.75 us
  transfers between devices with their start and end apart: 3 -> 9, of which waited for: 2 -> 7; matrix products, arithmetic and copies ran while one was open for 1% -> 2% of each run, Pallas kernels for 0% -> 0%
where the time goes in v1:
time: 149 us; the launch traced here: 148 us
  blocking collectives  65.3 us (44%)
  waiting for transfers between devices  48.1 us (32%)
  between operations  13.5 us (9%)
  starting transfers between devices  9.05 us (6%)
  local copies, waits for them, and re-layouts  7.55 us (5%)
  matrix products  2.47 us (2%)
  other arithmetic  2.33 us (2%)
    unnamed x4, waiting for transfers between devices  36.8 us
    all_gather x1, blocking collectives, body(): lax.all_gather(second_arm, 'row', axis=1, tiled=True)  27 us
    all_gather x1, blocking collectives, body(): lax.all_gather(in_second, 'row', axis=1, tiled=True)  26.6 us
    psum x2, blocking collectives, finish(): lax.psum((jnp.sum(product_sum, axis=0), jnp.sum(product_sum * product_sum...  11.6 us
    ppermute x6, waiting for transfers between devices, prepare(): lax.ppermute(moving, 'ch', [(i, (i + 1) % devices) for i in range(devices)])  11.3 us
    unnamed x26, local copies, waits for them, and re-layouts  5.75 us
    all_to_all x1, starting transfers between devices, body(): lax.all_to_all(in_first, 'row', split_axis=2, concat_axis=1, tiled=True)  5.51 us
    ppermute x6, starting transfers between devices, prepare(): lax.ppermute(moving, 'ch', [(i, (i + 1) % devices) for i in range(devices)])  3.5 us
  transfers between devices with their start and end apart: 9, of which 7 were waited for; matrix products, arithmetic and copies ran while one was open for 2% of the time, Pallas kernels for 0%

profile of v1, /device:TPU:0, one launch (start us, length us, event | category | flops | bytes accessed | tf_op | source)
XLA Modules:
  0.0 148.3 jit_solution(5572508416028550991)
XLA Ops:
  6.5 0.0 reduce-scatter.7.cloned.1.call-start
  6.5 0.5 collective-permute-start
  7.0 0.0 copy-start.9
  7.0 0.7 copy-done.9
  7.7 0.0 copy-start.1
  7.7 0.7 copy-done.1
  8.4 0.0 copy-start.2
  8.4 0.0 copy-start.3
  8.4 0.7 copy-done.2
  9.0 0.0 copy-done.3
  9.1 0.0 copy-start.5
  9.1 0.0 copy-start.4
  9.1 0.6 dynamic_slice.10
  9.7 0.1 copy-done.5
  9.7 0.0 copy-done.4
  9.8 0.6 broadcast_multiply_fusion
  10.4 0.0 collective-permute-done
  10.5 2.7 %collective-permute-start.1 = (bf16[32,1,8]{0,2,1:T(8,128)(2,1)S(1)}, bf16[32,1,8]{0,2,1:T(8,128)(2,1)S(1)}, u32[]{:S(2)}, u32[]{:S(2)}) collective-permute-start(bf16[32,1,8]{0,2,1:T(8,128)(2,1)S(1)} %collective-permute-done), channel_id=1, source_target_pairs={{0,1},{1,2},{2,3},{3,0},{4,5},{5,6},{6,7},{7,4},{8,9},{9,10},{10,1... | collective-permute-start | bytes 1544 | tf_op jit(solution)/shard_map/ppermute | solution.py:23
  13.1 0.8 collective-permute-done.1
  13.9 0.3 collective-permute-start.2
  14.3 0.7 copy-done.10
  14.9 0.6 dynamic_slice.9
  15.5 1.4 collective-permute-done.2
  16.9 0.0 copy-done
  16.9 0.2 convert_reduce_fusion.1
  17.2 0.9 convolution_bitcast_fusion.1
  18.1 0.1 fusion.56
  18.2 0.1 fusion.92
  18.2 27.0 %all_gather.6 = bf16[32,8,8]{0,2,1:T(8,128)(2,1)S(1)} all-gather(bf16[32,1,8]{0,2,1:T(8,128)(2,1)S(1)} %fusion.56), channel_id=1, replica_groups=mesh['row'=8,'ch'=4] {'row'}, dimensions={1}, use_global_device_ids=true | all-gather | bytes 4608 | tf_op jit(solution)/shard_map/all_gather | solution.py:89
  45.3 0.0 copy-start.7
  45.3 0.1 fusion.98
  45.5 5.7 %all-reduce.1 = (f32[1,8]{1,0:T(1,128)S(1)}, f32[1,8]{1,0:T(1,128)S(1)}) all-reduce(f32[1,8]{1,0:T(1,128)S(1)} %bitcast.174, f32[1,8]{1,0:T(1,128)S(1)} %bitcast.173), channel_id=1, replica_groups=mesh['row'=8,'ch'=4] {'ch'}, use_global_device_ids=true, to_apply=%region_5.7 | all-reduce | flops 16 | bytes 128 | tf_op jit(solution)/shard_map/psum | solution.py:42
  51.1 0.0 copy-done.7
  51.1 0.2 fusion.18
  51.3 0.7 copy.28
  52.0 0.0 reduce-scatter.7.cloned.1.call-update
  52.1 0.7 compare_convert_fusion
  52.7 18.7 %reduce-scatter.7.cloned.1.call-done = bf16[32,8]{1,0:T(8,128)(2,1)} async-done(((bf16[128,8]{1,0:T(8,128)(2,1)}), bf16[32,8]{1,0:T(8,128)(2,1)}) %reduce-scatter.7.cloned.1.call-update) | async-done | bytes 528
  71.4 0.8 copy.29
  72.2 0.0 copy-done.8
  72.2 0.2 fusion.17
  72.4 0.0 collective-permute-start.3
  72.4 3.0 %collective-permute-done.3 = bf16[32,1,8]{0,2,1:T(8,128)(2,1)S(1)} collective-permute-done((bf16[32,1,8]{0,2,1:T(8,128)(2,1)S(1)}, bf16[32,1,8]{0,2,1:T(8,128)(2,1)S(1)}, u32[]{:S(2)}, u32[]{:S(2)}) %collective-permute-start.3) | collective-permute-done | bytes 544 | tf_op jit(solution)/shard_map/ppermute | solution.py:23
  75.4 0.0 collective-permute-start.4
  75.4 3.0 %collective-permute-done.4 = bf16[32,1,8]{0,2,1:T(8,128)(2,1)S(1)} collective-permute-done((bf16[32,1,8]{0,2,1:T(8,128)(2,1)S(1)}, bf16[32,1,8]{0,2,1:T(8,128)(2,1)S(1)}, u32[]{:S(2)}, u32[]{:S(2)}) %collective-permute-start.4) | collective-permute-done | bytes 544 | tf_op jit(solution)/shard_map/ppermute | solution.py:23
  78.4 0.0 collective-permute-start.5
  78.4 3.0 %collective-permute-done.5 = bf16[32,1,8]{0,2,1:T(8,128)(2,1)S(1)} collective-permute-done((bf16[32,1,8]{0,2,1:T(8,128)(2,1)S(1)}, bf16[32,1,8]{0,2,1:T(8,128)(2,1)S(1)}, u32[]{:S(2)}, u32[]{:S(2)}) %collective-permute-start.5) | collective-permute-done | bytes 544 | tf_op jit(solution)/shard_map/ppermute | solution.py:23
  81.4 0.2 convert_reduce_fusion
  81.6 0.0 copy-done.6
  81.7 0.2 convolution_bitcast_fusion
  81.8 0.1 fusion.50
  81.9 0.6 copy.14
  82.5 5.5 %all-to-all-start = ((bf16[32,1,8]{0,1,2:T(2,128)(2,1)}), bf16[32,1,8]{0,1,2:T(2,128)(2,1)S(1)}, u32[]{:S(2)}, u32[]{:S(2)}) async-start(bf16[32,1,8]{0,1,2:T(2,128)(2,1)} %copy.14), calls=%async_computation | async-start | bytes 8192 | tf_op jit(solution)/shard_map/all_to_all | solution.py:98
  88.0 0.0 reduce-scatter.9.cloned.1.call-start
  88.1 26.6 %all_gather.7 = bf16[32,8,8]{0,2,1:T(8,128)(2,1)S(1)} all-gather(bf16[32,1,8]{0,2,1:T(8,128)(2,1)S(1)} %get-tuple-element.21), channel_id=1, replica_groups=mesh['row'=8,'ch'=4] {'row'}, dimensions={1}, use_global_device_ids=true | all-gather | bytes 4608 | tf_op jit(solution)/shard_map/all_gather | solution.py:103
  114.7 0.0 all-to-all-done
  114.7 0.1 fusion.97
  114.9 5.9 %all-reduce = (f32[1,8]{1,0:T(1,128)S(1)}, f32[1,8]{1,0:T(1,128)S(1)}) all-reduce(f32[1,8]{1,0:T(1,128)S(1)} %bitcast.176, f32[1,8]{1,0:T(1,128)S(1)} %bitcast.175), channel_id=1, replica_groups=mesh['row'=8,'ch'=4] {'ch'}, use_global_device_ids=true, to_apply=%region_12.14 | all-reduce | flops 16 | bytes 128 | tf_op jit(solution)/shard_map/psum | solution.py:42
  120.8 0.2 fusion.19
  121.0 0.7 copy.30
  121.7 0.0 reduce-scatter.9.cloned.1.call-update
  121.8 18.1 %reduce-scatter.9.cloned.1.call-done = bf16[32,8]{1,0:T(8,128)(2,1)} async-done(((bf16[128,8]{1,0:T(8,128)(2,1)}), bf16[32,8]{1,0:T(8,128)(2,1)}) %reduce-scatter.9.cloned.1.call-update) | async-done | bytes 528
  139.9 0.8 copy.31
  140.7 0.8 fusion.16
  (15 shorter events, 0.1 us)
Async XLA Ops:
  6.5 64.8 %reduce-scatter.7.cloned.1.call-start = ((), (), s32[]{:S(2)}) async-start(), calls=%async_computation.3 | async-start | bytes 40960
  6.5 3.9 %collective-permute-start = (bf16[32,1,8]{0,2,1:T(8,128)(2,1)}, bf16[32,1,8]{0,2,1:T(8,128)(2,1)S(1)}, u32[]{:S(2)}, u32[]{:S(2)}) collective-permute-start(bf16[32,1,8]{0,2,1:T(8,128)(2,1)} %param.13), channel_id=1, source_target_pairs={{0,1},{1,2},{2,3},{3,0},{4,5},{5,6},{6,7},{7,4},{8,9},{9,10},{10,1... | collective-permute-start | bytes 1544 | tf_op jit(solution)/shard_map/ppermute | solution.py:23
  7.0 0.7 copy-start.9
  7.7 0.7 copy-start.1
  8.4 0.7 copy-start.2
  8.4 0.7 copy-start.3
  9.1 0.7 copy-start.5
  9.1 0.7 copy-start.4
  10.5 3.5 %collective-permute-start.1 = (bf16[32,1,8]{0,2,1:T(8,128)(2,1)S(1)}, bf16[32,1,8]{0,2,1:T(8,128)(2,1)S(1)}, u32[]{:S(2)}, u32[]{:S(2)}) collective-permute-start(bf16[32,1,8]{0,2,1:T(8,128)(2,1)S(1)} %collective-permute-done), channel_id=1, source_target_pairs={{0,1},{1,2},{2,3},{3,0},{4,5},{5,6},{6,7},{7,4},{8,9},{9,10},{10,1... | collective-permute-start | bytes 1544 | tf_op jit(solution)/shard_map/ppermute | solution.py:23
  13.9 3.0 %collective-permute-start.2 = (bf16[32,1,8]{0,2,1:T(8,128)(2,1)S(1)}, bf16[32,1,8]{0,2,1:T(8,128)(2,1)S(1)}, u32[]{:S(2)}, u32[]{:S(2)}) collective-permute-start(bf16[32,1,8]{0,2,1:T(8,128)(2,1)S(1)} %collective-permute-done.1), channel_id=1, source_target_pairs={{0,1},{1,2},{2,3},{3,0},{4,5},{5,6},{6,7},{7,4},{8,9},{9,10},{10,1... | collective-permute-start | bytes 1544 | tf_op jit(solution)/shard_map/ppermute | solution.py:23
  14.3 0.7 copy-start.10
  14.9 2.0 %copy-start = (bf16[32,1,8]{0,2,1:T(8,128)(2,1)S(1)}, bf16[32,1,8]{0,2,1:T(8,128)(2,1)}, u32[]{:S(2)}) copy-start(bf16[32,1,8]{0,2,1:T(8,128)(2,1)} %param.13) | copy-start | bytes 1540
  45.3 5.8 %copy-start.7 = (bf16[2,32,128]{2,1,0:T(8,128)(2,1)S(1)}, bf16[2,32,128]{2,1,0:T(8,128)(2,1)}, u32[]{:S(2)}) copy-start(bf16[2,32,128]{2,1,0:T(8,128)(2,1)} %param.23) | copy-start | bytes 49156
  52.0 20.1 %copy-start.8 = (bf16[2,128,32]{1,2,0:T(8,128)(2,1)S(1)}, bf16[2,128,32]{1,2,0:T(8,128)(2,1)}, u32[]{:S(2)}) copy-start(bf16[2,128,32]{1,2,0:T(8,128)(2,1)} %param.19) | copy-start | bytes 49156
  72.2 9.5 %copy-start.6 = (bf16[2,128,4,32]{1,3,2,0:T(8,128)(2,1)S(1)}, bf16[2,128,4,32]{1,3,2,0:T(8,128)(2,1)}, u32[]{:S(2)}) copy-start(bf16[2,128,4,32]{1,3,2,0:T(8,128)(2,1)} %param.18) | copy-start | bytes 196612
  72.4 3.0 %collective-permute-start.3 = (bf16[32,1,8]{0,2,1:T(8,128)(2,1)S(1)}, bf16[32,1,8]{0,2,1:T(8,128)(2,1)S(1)}, u32[]{:S(2)}, u32[]{:S(2)}) collective-permute-start(bf16[32,1,8]{0,2,1:T(8,128)(2,1)S(1)} %fusion.17), channel_id=1, source_target_pairs={{0,1},{1,2},{2,3},{3,0},{4,5},{5,6},{6,7},{7,4},{8,9},{9,10},{10,1... | collective-permute-start | bytes 1544 | tf_op jit(solution)/shard_map/ppermute | solution.py:23
  75.4 3.0 %collective-permute-start.4 = (bf16[32,1,8]{0,2,1:T(8,128)(2,1)S(1)}, bf16[32,1,8]{0,2,1:T(8,128)(2,1)S(1)}, u32[]{:S(2)}, u32[]{:S(2)}) collective-permute-start(bf16[32,1,8]{0,2,1:T(8,128)(2,1)S(1)} %collective-permute-done.3), channel_id=1, source_target_pairs={{0,1},{1,2},{2,3},{3,0},{4,5},{5,6},{6,7},{7,4},{8,9},{9,10},{10,1... | collective-permute-start | bytes 1544 | tf_op jit(solution)/shard_map/ppermute | solution.py:23
  78.4 3.0 %collective-permute-start.5 = (bf16[32,1,8]{0,2,1:T(8,128)(2,1)S(1)}, bf16[32,1,8]{0,2,1:T(8,128)(2,1)S(1)}, u32[]{:S(2)}, u32[]{:S(2)}) collective-permute-start(bf16[32,1,8]{0,2,1:T(8,128)(2,1)S(1)} %collective-permute-done.4), channel_id=1, source_target_pairs={{0,1},{1,2},{2,3},{3,0},{4,5},{5,6},{6,7},{7,4},{8,9},{9,10},{10,1... | collective-permute-start | bytes 1544 | tf_op jit(solution)/shard_map/ppermute | solution.py:23
  82.5 32.2 %all-to-all-start = ((bf16[32,1,8]{0,1,2:T(2,128)(2,1)}), bf16[32,1,8]{0,1,2:T(2,128)(2,1)S(1)}, u32[]{:S(2)}, u32[]{:S(2)}) async-start(bf16[32,1,8]{0,1,2:T(2,128)(2,1)} %copy.14), calls=%async_computation | async-start | bytes 8192 | tf_op jit(solution)/shard_map/all_to_all | solution.py:98
  88.0 51.9 %reduce-scatter.9.cloned.1.call-start = ((), (), s32[]{:S(2)}) async-start(), calls=%async_computation.4 | async-start | bytes 40960
Sparse Core Ops, SparseCore 0:
  52.2 19.1 reduce-scatter.6
  121.9 17.9 reduce-scatter.8
